TPU v7x, 32 devices: a whole 2x2x4 slice. The times are simulated.
32 devices in a mesh: shot: 16 (over z, y, core), rcv: 2 (over x).
Axes of the slice: x: 2, y: 2, z: 4, core: 2. Of those that a mesh axis runs over, the one named last changes fastest.
Arguments:
- record: bfloat16 [768, 131072], P('rcv', 'shot'), may hold values from -6 to 6
- shot_fire_samples: int32 [512], P('shot'), may hold values from 0 to 131071, as said below
Outputs:
- psf_gram: float32 [2, 4, 768, 768], P(None, None, 'rcv', 'shot')
Inputs may be any that keep to these rules, and one draw needn't show every extreme that they name: `shot_fire_samples`: shot s fires at a sample from s * 256 to s * 256 + 255.
All inputs are finite; a program needn't handle non-finite values.
Results may differ from a plain program's by a relative error of at most 0.0025.
Values may be sent and summed in bfloat16 or wider, within the bound.
A program may use at most 64 MiB of HBM per device.

v0:
```python
import math
import jax
import jax.numpy as jnp
from jax import lax
from jax.sharding import PartitionSpec as P

WIN = 2048
SPACING = 256
freq_bins = (24, 40, 56, 80)


def shifted(block, axis, distance):
    devices = range(lax.axis_size(axis))
    route = [(i - distance, i) for i in devices if i - distance in devices]
    return lax.ppermute(block, axis, route)


def dft_table(window_len):
    lag_index = jnp.arange(window_len, dtype=jnp.int32)
    bin_list = jnp.array(freq_bins, dtype=jnp.int32)
    turn_count = lag_index[:, None] * bin_list[None, :] % window_len
    phase_angle = 2.0 * math.pi / window_len * turn_count.astype(jnp.float32)
    dft_rows = jnp.concatenate([jnp.cos(phase_angle), -jnp.sin(phase_angle)], axis=1) / math.sqrt(
        window_len
    )
    return dft_rows.astype(jnp.bfloat16)


def shifted_tables(jitter, span):
    lag_index = jnp.arange(span, dtype=jnp.int32)[None, :] - jitter[:, None]
    inside = (lag_index >= 0) & (lag_index < WIN)
    clipped = jnp.clip(lag_index, 0, WIN - 1)
    bin_list = jnp.array(freq_bins, dtype=jnp.int32)
    turn_count = clipped[:, None, :] * bin_list[None, :, None] % WIN
    phase_angle = 2.0 * math.pi / WIN * turn_count.astype(jnp.float32)
    table = jnp.concatenate([jnp.cos(phase_angle), -jnp.sin(phase_angle)], axis=1) / math.sqrt(WIN)
    table = jnp.where(inside[:, None, :], table, 0.0)
    return table.astype(jnp.bfloat16)


def local_spectra(extended, sample_offsets, dft_rows):
    count_of_shots = sample_offsets.shape[0]
    reach_blocks = WIN // SPACING + 1
    jitter = sample_offsets - jnp.arange(count_of_shots, dtype=jnp.int32) * SPACING
    tables = shifted_tables(jitter, reach_blocks * SPACING)
    tables = tables.reshape(count_of_shots, dft_rows.shape[1], reach_blocks, SPACING)
    blocks = extended.reshape(extended.shape[0], extended.shape[1] // SPACING, SPACING)
    total = jnp.zeros((count_of_shots, dft_rows.shape[1], extended.shape[0]), jnp.float32)
    for offset in range(reach_blocks):
        record_part = blocks[:, offset : offset + count_of_shots, :]
        total = total + jnp.einsum(
            "rsu,scu->scr", record_part, tables[:, :, offset, :], preferred_element_type=jnp.float32
        )
    return total


def gram_terms(left, right):
    nfreq = len(freq_bins)
    left_re = left[:, :nfreq, :]
    left_im = left[:, nfreq:, :]
    right_re = right[:, :nfreq, :]
    right_im = right[:, nfreq:, :]
    gram_real = jnp.einsum("sfr,sfq->frq", left_re, right_re, preferred_element_type=jnp.float32)
    gram_real = gram_real + jnp.einsum(
        "sfr,sfq->frq", left_im, right_im, preferred_element_type=jnp.float32
    )
    gram_imag = jnp.einsum("sfr,sfq->frq", left_re, right_im, preferred_element_type=jnp.float32)
    gram_imag = gram_imag - jnp.einsum(
        "sfr,sfq->frq", left_im, right_re, preferred_element_type=jnp.float32
    )
    return jnp.stack([gram_real, gram_imag], axis=0)


def per_device(record, shot_fire_samples):
    trace_segment_length = record.shape[1]
    count_of_shots = shot_fire_samples.shape[0]
    dft_rows = dft_table(WIN)
    sample_offsets = shot_fire_samples - lax.axis_index("shot") * trace_segment_length
    head_rows = record[:, :WIN]
    rim_rows = shifted(head_rows, "shot", -1)
    extended = jnp.concatenate([record, rim_rows], axis=1)
    trace_spectra = local_spectra(extended, sample_offsets, dft_rows)
    trace_spectra = trace_spectra.astype(jnp.bfloat16)
    all_receivers = lax.all_gather(trace_spectra, "rcv", axis=2, tiled=True)
    total_shots = count_of_shots * lax.axis_size("shot")
    row_side = lax.all_gather(trace_spectra, "shot", axis=0, tiled=True)
    column_side = lax.all_to_all(all_receivers, "shot", split_axis=2, concat_axis=0, tiled=True)
    result = gram_terms(row_side, column_side)
    return result / total_shots


def solution(mesh):
    return jax.shard_map(
        per_device,
        mesh=mesh,
        in_specs=(P("rcv", "shot"), P("shot")),
        out_specs=P(None, None, "rcv", "shot"),
        check_vma=False,
    )
```

profile of v0, /device:TPU:0, one launch (start us, length us, event | category | flops | bytes accessed | tf_op | source)
XLA Modules:
  0.0 125.5 jit_solution(16879435166929564003)
XLA Ops:
  6.5 0.0 all-gather.2.cloned.1.call-start
  6.5 8.6 %copy.41 = bf16[384,8192]{0,1:T(8,128)(2,1)} copy(bf16[384,8192]{1,0:T(8,128)(2,1)} %param.3) | data formatting | bytes 12582912 | tf_op args[0]
  15.2 0.0 copy-start.2
  15.2 0.0 copy-start.1
  15.2 1.6 %slice.93 = bf16[384,2048]{0,1:T(8,128)(2,1)S(1)} slice(bf16[384,8192]{0,1:T(8,128)(2,1)} %copy.41), slice={[0:384], [0:2048]} | slice | bytes 3145728 | tf_op jit(solution)/shard_map/slice | solution.py:79
  16.8 1.3 %collective-permute-start = (bf16[384,2048]{0,1:T(8,128)(2,1)S(1)}, bf16[384,2048]{0,1:T(8,128)(2,1)S(1)}, u32[]{:S(2)}, u32[]{:S(2)}) collective-permute-start(bf16[384,2048]{0,1:T(8,128)(2,1)S(1)} %slice.93), channel_id=1, source_target_pairs={{2,0},{4,2},{6,4},{8,6},{10,8},{12,10},{14,12},{16,14},{18,16},{20... | collective-permute-start | bytes 4718600 | tf_op jit(solution)/shard_map/ppermute | solution.py:15
  18.1 0.0 copy-done.2
  18.1 0.1 fusion.71
  18.3 0.0 copy-start
  18.3 0.1 subtract_clamp_fusion
  18.4 0.0 copy-done.1
  18.4 9.7 %fusion.70 = (f32[32,4,9,256]{3,1,0,2:T(4,128)S(1)}, f32[32,4,9,256]{3,1,0,2:T(4,128)S(1)}) fusion(s32[4]{0:T(128)S(1)} %copy-done.1, s32[32,9,256]{2,0,1:T(8,128)S(1)} %subtract_clamp_fusion), kind=kLoop, calls=%fused_computation.54 | loop fusion | flops 4423680 | bytes 2654224 | tf_op jit(solution)/shard_map/cos | solution.py:36
  28.1 0.8 fusion.19
  29.0 0.0 collective-permute-done
  29.0 0.0 copy-done
  29.0 14.8 %pad_maximum_fusion = bf16[384,10240]{0,1:T(8,128)(2,1)S(1)} fusion(bf16[384,2048]{0,1:T(8,128)(2,1)S(1)} %collective-permute-done, bf16[384,8192]{0,1:T(8,128)(2,1)S(1)} %copy-done), kind=kLoop, calls=%fused_computation | loop fusion | flops 15728640 | bytes 15728640 | tf_op jit(solution)/shard_map/concatenate | solution.py:81
  43.9 0.9 fusion
  44.8 0.9 fusion.2
  45.7 0.9 fusion.4
  46.6 0.9 fusion.6
  47.6 0.9 fusion.8
  48.5 0.9 fusion.10
  49.4 0.9 fusion.12
  50.4 0.9 fusion.14
  51.3 1.6 %fusion.55 = bf16[32,8,384]{2,1,0:T(8,128)(2,1)} fusion(f32[32,8,384]{2,1,0:T(8,128)S(1)} %fusion, f32[32,8,384]{2,1,0:T(8,128)S(1)} %fusion.2, f32[32,8,384]{2,1,0:T(8,128)S(1)} %fusion.4, f32[32,8,384]{2,1,0:T(8,128)S(1)} %fusion.6, f32[32,8,384]{2,1,0:T(8,128)S(1)} %fusion.8, f32[32,8,384]{2,1,0:T(8,128)S(1)} %fusion.10, f32[32,8,384]{2,1,0:T(8,128)S(1)} %fusion.12, ...), kind=kOutput, calls=%fused_computation.48 | convolution fusion | flops 51216384 | bytes 9764864 | tf_op jit(solution)/shard_map/rsu,scu->scr/dot_general | solution.py:51
  52.9 0.0 all-gather.2.cloned.1.call-update
  52.9 7.5 %all_gather.7 = bf16[32,8,768]{2,1,0:T(8,128)(2,1)S(1)} all-gather(bf16[32,8,384]{2,1,0:T(8,128)(2,1)} %fusion.55), channel_id=1, replica_groups=mesh['shot'=16,'rcv'=2] {'rcv'}, dimensions={2}, use_global_device_ids=true | all-gather | bytes 589824 | tf_op jit(solution)/shard_map/all_gather | solution.py:84
  60.5 1.2 copy.52
  61.6 1.5 %reshape.59 = bf16[16,2,6144]{2,1,0:T(2,128)(2,1)S(1)} reshape(bf16[768,8,32]{2,1,0:T(8,128)(2,1)S(1)} %bitcast.53) | data formatting | bytes 786432
  63.1 28.9 %all_to_all.18 = bf16[16,2,6144]{2,1,0:T(2,128)(2,1)S(1)} all-to-all(bf16[16,2,6144]{2,1,0:T(2,128)(2,1)S(1)} %reshape.59), channel_id=1, replica_groups=mesh['shot'=16,'rcv'=2] {'shot'}, dimensions={0} | all-to-all | bytes 786432 | tf_op jit(solution)/shard_map/all_to_all | solution.py:87
  92.1 0.8 reshape.60
  92.8 1.0 copy.83
  93.8 1.5 %all_to_all.16 = bf16[512,8,48]{0,2,1:T(8,128)(2,1)S(1)} reshape(bf16[16,32,8,48]{1,0,3,2:T(8,128)(2,1)S(1)} %bitcast.52) | data formatting | bytes 786432 | tf_op jit(solution)/shard_map/all_to_all | solution.py:87
  95.3 16.9 %all-gather.2.cloned.1.call-done = bf16[512,8,384]{2,1,0:T(8,128)(2,1)} async-done(((bf16[32,8,384]{2,1,0:T(8,128)(2,1)}), bf16[512,8,384]{2,1,0:T(8,128)(2,1)}) %all-gather.2.cloned.1.call-update) | async-done | bytes 3145744 | tf_op jit(solution)/shard_map/all_gather | solution.py:86
  112.3 4.1 %fusion.76 = (bf16[512,4,384]{2,1,0:T(4,128)(2,1)S(1)}, bf16[512,4,384]{2,1,0:T(4,128)(2,1)S(1)}) fusion(bf16[512,8,384]{2,1,0:T(8,128)(2,1)} %all-gather.2.cloned.1.call-done), kind=kLoop, calls=%fused_computation.74 | loop fusion | bytes 6291456 | tf_op jit(solution)/shard_map/slice | solution.py:59
  116.3 0.4 fusion.22
  116.7 0.4 fusion.20
  117.1 0.4 fusion.67
  117.4 0.4 fusion.64
  117.8 0.9 maximum_multiply_fusion.1
  (2 shorter events, 0.0 us)
Async XLA Ops:
  6.5 105.7 %all-gather.2.cloned.1.call-start = ((), (), s32[]{:S(2)}) async-start(), calls=%async_computation.1 | async-start | bytes 3342336 | tf_op jit(solution)/shard_map/all_gather | solution.py:86
  15.2 2.9 %copy-start.2 = (s32[32]{0:T(128)S(1)}, s32[32]{0:T(128)}, u32[]{:S(2)}) copy-start(s32[32]{0:T(128)} %param.4) | copy-start | bytes 388
  15.2 3.2 %copy-start.1 = (s32[4]{0:T(128)S(1)}, s32[4]{0:T(128)}, u32[]{:S(2)}) copy-start(s32[4]{0:T(128)} %constant.43.clone) | copy-start | bytes 52
  16.8 12.2 %collective-permute-start = (bf16[384,2048]{0,1:T(8,128)(2,1)S(1)}, bf16[384,2048]{0,1:T(8,128)(2,1)S(1)}, u32[]{:S(2)}, u32[]{:S(2)}) collective-permute-start(bf16[384,2048]{0,1:T(8,128)(2,1)S(1)} %slice.93), channel_id=1, source_target_pairs={{2,0},{4,2},{6,4},{8,6},{10,8},{12,10},{14,12},{16,14},{18,16},{20... | collective-permute-start | bytes 4718600 | tf_op jit(solution)/shard_map/ppermute | solution.py:15
  18.3 10.8 %copy-start = (bf16[384,8192]{0,1:T(8,128)(2,1)S(1)}, bf16[384,8192]{0,1:T(8,128)(2,1)}, u32[]{:S(2)}) copy-start(bf16[384,8192]{0,1:T(8,128)(2,1)} %copy.41) | copy-start | bytes 18874372
Sparse Core Ops, SparseCore 0:
  53.0 59.1 all-gather.1
where the time goes:
time: 126 us
  blocking collectives  36.5 us (29%)
  other arithmetic  26.6 us (21%)
  local copies, waits for them, and re-layouts  20.2 us (16%)
  waiting for transfers between devices  17 us (13%)
  between operations  13.6 us (11%)
  matrix products  10.5 us (8%)
  starting transfers between devices  1.29 us (1%)
    all_to_all x1, blocking collectives, per_device(): lax.all_to_all(all_receivers, 'shot', split_axis=2, concat_axis=0, tiled=...  28.9 us
    all_gather x1, waiting for transfers between devices, per_device(): row_side = lax.all_gather(trace_spectra, 'shot', axis=0, tiled=True)  16.9 us
    concatenate x1, other arithmetic, per_device(): extended = jnp.concatenate([record, rim_rows], axis=1)  14.8 us
    unnamed x9, local copies, waits for them, and re-layouts  10.9 us
    cos x1, other arithmetic, shifted_tables(): jnp.cos(phase_angle)  9.74 us
    dot_general x9, matrix products, local_spectra(): jnp.einsum('rsu,scu->scr', record_part, tables[:, :, offset, :], preferre...  9.03 us
    all_gather x1, blocking collectives, per_device(): all_receivers = lax.all_gather(trace_spectra, 'rcv', axis=2, tiled=True)  7.55 us
    slice x1, local copies, waits for them, and re-layouts, gram_terms(): left_re = left[:, :nfreq, :]  4.06 us
  transfers between devices with their start and end apart: 2, of which 1 were waited for; matrix products, arithmetic and copies ran while one was open for 12% of the time, Pallas kernels for 0%

commit v1 on v0

--- a/solution.py
+++ b/solution.py
@@ -81,7 +81,7 @@
     extended = jnp.concatenate([record, rim_rows], axis=1)
     trace_spectra = local_spectra(extended, sample_offsets, dft_rows)
     trace_spectra = trace_spectra.astype(jnp.bfloat16)
-    all_receivers = lax.all_gather(trace_spectra, "rcv", axis=2, tiled=True)
+    all_receivers = jnp.concatenate(lax.all_gather(trace_spectra, "rcv"), axis=2)
     total_shots = count_of_shots * lax.axis_size("shot")
     row_side = lax.all_gather(trace_spectra, "shot", axis=0, tiled=True)
     column_side = lax.all_to_all(all_receivers, "shot", split_axis=2, concat_axis=0, tiled=True)

time: 126 us -> 126 us (level)
    reshape x0 -> x1, local copies, waits for them, and re-layouts: none -> 1.34 us  [per_device(): jnp.concatenate(lax.all_gather(trace_spectra, 'rcv'), axis=2)]
  transfers between devices with their start and end apart: 2 -> 2, of which waited for: 1 -> 1; matrix products, arithmetic and copies ran while one was open for 12% -> 13% of each run, Pallas kernels for 0% -> 0%
where the time goes in v1:
time: 126 us
  blocking collectives  36.5 us (29%)
  other arithmetic  26.6 us (21%)
  local copies, waits for them, and re-layouts  20.8 us (17%)
  waiting for transfers between devices  16.5 us (13%)
  between operations  13.6 us (11%)
  matrix products  10.5 us (8%)
  starting transfers between devices  1.29 us (1%)
    all_to_all x1, blocking collectives, per_device(): lax.all_to_all(all_receivers, 'shot', split_axis=2, concat_axis=0, tiled=...  28.9 us
    all_gather x1, waiting for transfers between devices, per_device(): row_side = lax.all_gather(trace_spectra, 'shot', axis=0, tiled=True)  16.5 us
    concatenate x1, other arithmetic, per_device(): extended = jnp.concatenate([record, rim_rows], axis=1)  14.8 us
    unnamed x9, local copies, waits for them, and re-layouts  10.9 us
    cos x1, other arithmetic, shifted_tables(): jnp.cos(phase_angle)  9.74 us
    dot_general x9, matrix products, local_spectra(): jnp.einsum('rsu,scu->scr', record_part, tables[:, :, offset, :], preferre...  9.03 us
    all_gather x1, blocking collectives, per_device(): lax.all_gather(trace_spectra, 'rcv')  7.55 us
    slice x1, local copies, waits for them, and re-layouts, gram_terms(): left_re = left[:, :nfreq, :]  4.06 us
  transfers between devices with their start and end apart: 2, of which 1 were waited for; matrix products, arithmetic and copies ran while one was open for 13% of the time, Pallas kernels for 0%

profile of v1, /device:TPU:0, one launch (start us, length us, event | category | flops | bytes accessed | tf_op | source)
XLA Modules:
  0.0 125.7 jit_solution(13506873950316850135)
XLA Ops:
  6.5 0.0 all-gather.3.cloned.1.call-start
  6.5 8.6 %copy.43 = bf16[384,8192]{0,1:T(8,128)(2,1)} copy(bf16[384,8192]{1,0:T(8,128)(2,1)} %param.3) | data formatting | bytes 12582912 | tf_op args[0]
  15.2 0.0 copy-start.2
  15.2 0.0 copy-start.1
  15.2 1.6 %slice.93 = bf16[384,2048]{0,1:T(8,128)(2,1)S(1)} slice(bf16[384,8192]{0,1:T(8,128)(2,1)} %copy.43), slice={[0:384], [0:2048]} | slice | bytes 3145728 | tf_op jit(solution)/shard_map/slice | solution.py:79
  16.8 1.3 %collective-permute-start = (bf16[384,2048]{0,1:T(8,128)(2,1)S(1)}, bf16[384,2048]{0,1:T(8,128)(2,1)S(1)}, u32[]{:S(2)}, u32[]{:S(2)}) collective-permute-start(bf16[384,2048]{0,1:T(8,128)(2,1)S(1)} %slice.93), channel_id=1, source_target_pairs={{2,0},{4,2},{6,4},{8,6},{10,8},{12,10},{14,12},{16,14},{18,16},{20... | collective-permute-start | bytes 4718600 | tf_op jit(solution)/shard_map/ppermute | solution.py:15
  18.1 0.0 copy-done.2
  18.1 0.1 fusion.71
  18.3 0.0 copy-start
  18.3 0.1 subtract_clamp_fusion
  18.4 0.0 copy-done.1
  18.4 9.7 %fusion.70 = (f32[32,4,9,256]{3,1,0,2:T(4,128)S(1)}, f32[32,4,9,256]{3,1,0,2:T(4,128)S(1)}) fusion(s32[4]{0:T(128)S(1)} %copy-done.1, s32[32,9,256]{2,0,1:T(8,128)S(1)} %subtract_clamp_fusion), kind=kLoop, calls=%fused_computation.53 | loop fusion | flops 4423680 | bytes 2654224 | tf_op jit(solution)/shard_map/cos | solution.py:36
  28.1 0.8 fusion.19
  29.0 0.0 collective-permute-done
  29.0 0.0 copy-done
  29.0 14.8 %pad_maximum_fusion = bf16[384,10240]{0,1:T(8,128)(2,1)S(1)} fusion(bf16[384,2048]{0,1:T(8,128)(2,1)S(1)} %collective-permute-done, bf16[384,8192]{0,1:T(8,128)(2,1)S(1)} %copy-done), kind=kLoop, calls=%fused_computation | loop fusion | flops 15728640 | bytes 15728640 | tf_op jit(solution)/shard_map/concatenate | solution.py:81
  43.9 0.9 fusion
  44.8 0.9 fusion.2
  45.7 0.9 fusion.4
  46.6 0.9 fusion.6
  47.6 0.9 fusion.8
  48.5 0.9 fusion.10
  49.4 0.9 fusion.12
  50.4 0.9 fusion.14
  51.3 1.6 %fusion.55 = bf16[32,8,384]{2,1,0:T(8,128)(2,1)} fusion(f32[32,8,384]{2,1,0:T(8,128)S(1)} %fusion, f32[32,8,384]{2,1,0:T(8,128)S(1)} %fusion.2, f32[32,8,384]{2,1,0:T(8,128)S(1)} %fusion.4, f32[32,8,384]{2,1,0:T(8,128)S(1)} %fusion.6, f32[32,8,384]{2,1,0:T(8,128)S(1)} %fusion.8, f32[32,8,384]{2,1,0:T(8,128)S(1)} %fusion.10, f32[32,8,384]{2,1,0:T(8,128)S(1)} %fusion.12, ...), kind=kOutput, calls=%fused_computation.47 | convolution fusion | flops 51216384 | bytes 9764864 | tf_op jit(solution)/shard_map/rsu,scu->scr/dot_general | solution.py:51
  52.9 0.0 all-gather.3.cloned.1.call-update
  52.9 7.5 %all-gather = bf16[64,8,384]{2,1,0:T(8,128)(2,1)S(1)} all-gather(bf16[32,8,384]{2,1,0:T(8,128)(2,1)} %fusion.55), channel_id=2, replica_groups=mesh['shot'=16,'rcv'=2] {'rcv'}, dimensions={0}, use_global_device_ids=true | all-gather | bytes 589824 | tf_op jit(solution)/shard_map/all_gather | solution.py:84
  60.5 0.4 copy.90
  60.9 1.3 %copy.59 = bf16[32,8,2,384]{0,1,3,2:T(8,128)(2,1)S(1)} copy(bf16[32,8,2,384]{3,2,1,0:T(2,128)(2,1)S(1)} %bitcast.59) | data formatting | bytes 786432 | tf_op jit(solution)/shard_map/reshape | solution.py:84
  62.2 1.5 %reshape.68 = bf16[16,2,6144]{2,1,0:T(2,128)(2,1)S(1)} reshape(bf16[768,8,32]{2,1,0:T(8,128)(2,1)S(1)} %bitcast.57) | data formatting | bytes 786432
  63.7 28.9 %all_to_all.18 = bf16[16,2,6144]{2,1,0:T(2,128)(2,1)S(1)} all-to-all(bf16[16,2,6144]{2,1,0:T(2,128)(2,1)S(1)} %reshape.68), channel_id=1, replica_groups=mesh['shot'=16,'rcv'=2] {'shot'}, dimensions={0} | all-to-all | bytes 786432 | tf_op jit(solution)/shard_map/all_to_all | solution.py:87
  92.7 0.8 reshape.69
  93.4 1.0 copy.57
  94.4 1.5 %all_to_all.16 = bf16[512,8,48]{0,2,1:T(8,128)(2,1)S(1)} reshape(bf16[16,32,8,48]{1,0,3,2:T(8,128)(2,1)S(1)} %copy.57) | data formatting | bytes 786432 | tf_op jit(solution)/shard_map/all_to_all | solution.py:87
  95.9 16.5 %all-gather.3.cloned.1.call-done = bf16[512,8,384]{2,1,0:T(8,128)(2,1)} async-done(((bf16[32,8,384]{2,1,0:T(8,128)(2,1)}), bf16[512,8,384]{2,1,0:T(8,128)(2,1)}) %all-gather.3.cloned.1.call-update) | async-done | bytes 3145744 | tf_op jit(solution)/shard_map/all_gather | solution.py:86
  112.5 4.1 %fusion.76 = (bf16[512,4,384]{2,1,0:T(4,128)(2,1)S(1)}, bf16[512,4,384]{2,1,0:T(4,128)(2,1)S(1)}) fusion(bf16[512,8,384]{2,1,0:T(8,128)(2,1)} %all-gather.3.cloned.1.call-done), kind=kLoop, calls=%fused_computation.74 | loop fusion | bytes 6291456 | tf_op jit(solution)/shard_map/slice | solution.py:59
  116.5 0.4 fusion.22
  116.9 0.4 fusion.20
  117.2 0.4 fusion.67
  117.6 0.4 fusion.64
  118.0 0.9 maximum_multiply_fusion.1
  (2 shorter events, 0.0 us)
Async XLA Ops:
  6.5 105.9 %all-gather.3.cloned.1.call-start = ((), (), s32[]{:S(2)}) async-start(), calls=%async_computation.1 | async-start | bytes 3342336 | tf_op jit(solution)/shard_map/all_gather | solution.py:86
  15.2 2.9 %copy-start.2 = (s32[32]{0:T(128)S(1)}, s32[32]{0:T(128)}, u32[]{:S(2)}) copy-start(s32[32]{0:T(128)} %param.4) | copy-start | bytes 388
  15.2 3.2 %copy-start.1 = (s32[4]{0:T(128)S(1)}, s32[4]{0:T(128)}, u32[]{:S(2)}) copy-start(s32[4]{0:T(128)} %constant.43.clone) | copy-start | bytes 52
  16.8 12.2 %collective-permute-start = (bf16[384,2048]{0,1:T(8,128)(2,1)S(1)}, bf16[384,2048]{0,1:T(8,128)(2,1)S(1)}, u32[]{:S(2)}, u32[]{:S(2)}) collective-permute-start(bf16[384,2048]{0,1:T(8,128)(2,1)S(1)} %slice.93), channel_id=1, source_target_pairs={{2,0},{4,2},{6,4},{8,6},{10,8},{12,10},{14,12},{16,14},{18,16},{20... | collective-permute-start | bytes 4718600 | tf_op jit(solution)/shard_map/ppermute | solution.py:15
  18.3 10.8 %copy-start = (bf16[384,8192]{0,1:T(8,128)(2,1)S(1)}, bf16[384,8192]{0,1:T(8,128)(2,1)}, u32[]{:S(2)}) copy-start(bf16[384,8192]{0,1:T(8,128)(2,1)} %copy.43) | copy-start | bytes 18874372
Sparse Core Ops, SparseCore 0:
  53.0 59.3 all-gather.2
